TPU v7x, 256 devices: a whole 4x4x8 slice. The times are simulated.
256 devices in a mesh: pairs: 64 (over z, x, core), win: 4 (over y).
Axes of the slice: x: 4, y: 4, z: 8, core: 2. Of those that a mesh axis runs over, the one named last changes fastest.
Arguments:
- raw_traces: bfloat16 [4, 320, 128, 512], P('win', None, 'pairs'), may hold values from -6 to 6
- tile_pairs: int32 [64, 4, 2], replicated, may hold values from -1 to 319, as said below
- block_slot: int32 [320], replicated, may hold values from 0 to 319, as said below
- win_offset: int32 [4], P('win'), may hold values from 0 to 128
Outputs:
- stacks: float32 [128, 256, 128, 128], P('win', 'pairs')
Inputs may be any that keep to these rules, and one draw needn't show every extreme that they name: `tile_pairs`: row p lists owner p's tiles: pairs of block numbers, then rows of -1. Each owner has 1 to 4 tiles and some owner exactly 4. The blocks named in one owner's row are all different. `block_slot`: each slot holds exactly one block.
All inputs are finite; a program needn't handle non-finite values.
Results may differ from a plain program's by a relative error of at most 0.0041.
Values may be sent and summed in bfloat16 or wider, within the bound.
A program may use at most 192 MiB of HBM per device.

v0:
```python
import math
import jax
import jax.numpy as jnp
from jax import lax
from jax.sharding import PartitionSpec as P

LAGS = 128
eps = 1e-06


def whiten(signal):
    length = signal.shape[-1]
    width = LAGS
    radius = LAGS // 2
    seg_count = length // width
    magnitude = jnp.abs(signal).reshape(signal.shape[:-1] + (seg_count, width))
    padded = jnp.pad(magnitude, [(0, 0)] * (magnitude.ndim - 2) + [(1, 1), (0, 0)])
    windows = jnp.concatenate([padded[..., :-2, :], padded[..., 1:-1, :], padded[..., 2:, :]], -1)
    rowpos = jnp.arange(3 * width)[:, None]
    colpos = jnp.arange(width)[None, :]
    band_matrix = (jnp.abs(rowpos - width - colpos) <= radius).astype(jnp.float32)
    totals = jnp.einsum(
        "...ni,ij->...nj", windows, band_matrix, precision=lax.Precision.HIGHEST
    ).reshape(signal.shape)
    position = jnp.arange(length)
    tally = (jnp.minimum(position, radius) + jnp.minimum(length - 1 - position, radius) + 1).astype(
        jnp.float32
    )
    return (signal / (totals / tally + eps)).astype(jnp.bfloat16)


def correlate(leading_blocks, trailing_blocks):
    seg_len = leading_blocks.shape[-1]
    samples = seg_len - LAGS
    half = LAGS // 2
    kernel = jnp.transpose(leading_blocks[..., half : half + samples], (1, 0, 2))
    source = jnp.transpose(trailing_blocks[..., : seg_len - 1], (1, 0, 2))
    return lax.conv_general_dilated(
        source,
        kernel,
        (1,),
        "VALID",
        dimension_numbers=("NCH", "OIH", "CNH"),
        preferred_element_type=jnp.float32,
    )


def body(raw_traces, tile_pairs, block_slot, win_offset):
    owner_index = lax.axis_index("pairs")
    pair_count = lax.axis_size("pairs")
    win_count = lax.axis_size("win")
    local_channels = raw_traces.shape[2]
    channels = local_channels * pair_count
    seg_len = raw_traces.shape[3] - LAGS
    samples = seg_len - LAGS
    tile_count = tile_pairs.shape[1]
    segment = lax.dynamic_slice_in_dim(raw_traces[0], win_offset[0], seg_len, 2).astype(jnp.float32)
    whitened = whiten(segment)
    wanted = tile_pairs.reshape(pair_count, 2 * tile_count)
    slot_index = block_slot[jnp.maximum(wanted, 0)]
    outgoing = jnp.take(whitened, slot_index.reshape(-1), axis=0).reshape(
        pair_count, 2 * tile_count, local_channels, seg_len
    )
    incoming = lax.all_to_all(outgoing, "pairs", split_axis=0, concat_axis=2, tiled=True)
    blocks = incoming[0].reshape(tile_count, 2, channels, seg_len)
    own_tiles = lax.dynamic_index_in_dim(tile_pairs, owner_index, 0, keepdims=False)
    tile_valid = (own_tiles[:, 0] >= 0).astype(jnp.float32)
    firsts = blocks[:, 0]
    seconds = blocks[:, 1]
    row_share = channels // win_count
    spread_rows = lax.all_to_all(firsts[:, None], "win", split_axis=2, concat_axis=1, tiled=True)
    initial = jnp.zeros((row_share, tile_count, channels, LAGS), jnp.float32)
    piece = lax.all_gather(seconds[:, None], "win", axis=1, tiled=True)
    summed = initial + jnp.stack(
        [correlate(spread_rows[tile], piece[tile]) for tile in range(tile_count)], 1
    )
    scale = 1.0 / math.sqrt(win_count * samples)
    return summed * scale * tile_valid[None, :, None, None]


def solution(mesh):
    return jax.shard_map(
        body,
        mesh=mesh,
        in_specs=(P("win", None, "pairs", None), P(), P(), P("win")),
        out_specs=P("win", "pairs", None, None),
        check_vma=False,
    )
```

profile of v0, /device:TPU:1, one launch (start us, length us, event | category | flops | bytes accessed | tf_op | source)
XLA Modules:
  0.0 132.8 jit_solution(15492690190346590132)
XLA Ops:
  6.5 0.0 copy-start
  6.5 0.0 copy-start.1
  6.5 0.0 all-gather.2.cloned.1.call-start
  7.3 0.7 broadcast_maximum_fusion
  8.0 0.1 copy.86
  8.1 0.2 reshape.108
  8.3 0.0 copy-done.1
  8.3 3.5 %gather_fusion = s32[512]{0:T(512)S(1)} fusion(s32[320]{0:T(512)S(1)} %copy-done.1, s32[1024]{0:T(1024)S(1)} %pad_clamp_fusion.1), kind=kCustom, calls=%fused_computation | custom fusion | bytes 6144 | tf_op jit(solution)/shard_map/gather | solution.py:60
  11.8 0.1 reshape.107
  11.9 0.0 copy-done
  11.9 0.9 constant_dynamic-slice_fusion.1
  12.8 0.1 convert_abs_fusion
  12.9 0.4 copy.88
  13.3 0.4 copy.89
  13.7 0.1 pad_slice_fusion.1
  13.8 1.8 %fusion = f32[320,2,3,128]{0,3,2,1:T(8,128)S(1)} fusion(f32[320,2,3,128]{3,0,2,1:T(8,128)S(1)} %get-tuple-element.10, f32[320,2,3,128]{3,0,2,1:T(8,128)S(1)} %copy.89, f32[320,2,3,128]{3,0,2,1:T(8,128)S(1)} %get-tuple-element.9, s32[384]{0:T(512)S(1)} %iota_add_fusion), kind=kOutput, calls=%fused_computation.3 | convolution fusion | flops 1134084096 | bytes 3933696 | tf_op jit(solution)/shard_map/...ni,ij->...nj/dot_general | solution.py:22
  15.7 0.3 copy.92
  16.0 0.2 fusion.7
  16.2 0.5 copy.93
  16.7 3.1 %gather_fusion.1 = bf16[512,2,384]{2,1,0:T(2,128)(2,1)S(1)} fusion(bf16[320,2,384]{2,1,0:T(2,128)(2,1)S(1)} %copy.93, s32[1024]{0:T(1024)S(1)} %pad_clamp_fusion), kind=kCustom, calls=%fused_computation.1 | custom fusion | bytes 1574912 | tf_op jit(solution)/shard_map/jit(_take)/gather | solution.py:61
  19.8 0.2 bitcast_select_fusion
  20.0 0.1 copy.95
  20.1 35.5 %all_to_all.24 = bf16[64,8,2,384]{3,1,2,0:T(8,128)(2,1)S(1)} all-to-all(bf16[64,8,2,384]{3,1,2,0:T(8,128)(2,1)S(1)} %copy.95), channel_id=1, replica_groups=mesh['pairs'=64,'win'=4] {'pairs'}, dimensions={0} | all-to-all | bytes 1572864 | tf_op jit(solution)/shard_map/all_to_all | solution.py:64
  55.7 0.3 reshape.126
  56.0 1.1 fusion.24
  57.1 0.0 copy-start.2
  57.1 0.8 copy.136
  57.9 0.0 all-gather.2.cloned.1.call-update
  57.9 0.9 copy.99
  58.9 4.2 %all-to-all-start.1 = ((bf16[4,1,128,384]{3,0,1,2:T(4,128)(2,1)}), bf16[4,1,128,384]{3,0,1,2:T(4,128)(2,1)S(1)}, u32[]{:S(2)}, u32[]{:S(2)}) async-start(bf16[4,1,128,384]{3,0,1,2:T(4,128)(2,1)} %copy.99), calls=%async_computation.1 | async-start | bytes 786432 | tf_op jit(solution)/shard_map/all_to_all | solution.py:71
  63.0 0.0 copy-done.2
  63.0 0.1 constant_dynamic-slice_fusion
  63.1 0.1 copy.111
  63.2 6.4 %all-to-all-done.1 = bf16[4,1,128,384]{3,0,1,2:T(4,128)(2,1)S(1)} async-done(((bf16[4,1,128,384]{3,0,1,2:T(4,128)(2,1)}), bf16[4,1,128,384]{3,0,1,2:T(4,128)(2,1)S(1)}, u32[]{:S(2)}, u32[]{:S(2)}) %all-to-all-start.1) | async-done | bytes 393248 | tf_op jit(solution)/shard_map/all_to_all | solution.py:71
  69.6 0.6 fusion.25
  70.2 0.1 slice.86
  70.3 0.1 slice.92
  70.4 0.1 slice.89
  70.5 0.1 slice.95
  70.6 0.2 copy.130
  70.8 0.2 copy.124
  71.0 0.2 copy.127
  71.2 0.9 copy.121
  72.1 12.6 %all-gather.2.cloned.1.call-done = bf16[4,4,128,384]{3,2,0,1:T(8,128)(2,1)} async-done(((bf16[4,1,128,384]{3,2,0,1:T(8,128)(2,1)}), bf16[4,4,128,384]{3,2,0,1:T(8,128)(2,1)}) %all-gather.2.cloned.1.call-update) | async-done | bytes 1572880 | tf_op jit(solution)/shard_map/all_gather | solution.py:73
  84.6 1.5 %fusion.23 = (bf16[1,4,128,384]{3,2,0,1:T(8,128)(2,1)S(1)}, bf16[1,4,128,384]{3,2,0,1:T(8,128)(2,1)S(1)}, bf16[1,4,128,384]{3,2,0,1:T(8,128)(2,1)S(1)}, bf16[1,4,128,384]{3,2,0,1:T(8,128)(2,1)S(1)}) fusion(bf16[4,4,128,384]{3,2,0,1:T(8,128)(2,1)} %all-gather.2.cloned.1.call-done), kind=kLoop, calls=%fused_computation.48 | loop fusion | bytes 3145728 | tf_op jit(solution)/shard_map/slice | solution.py:75
  86.2 0.2 copy.118
  86.4 0.2 copy.125
  86.7 0.2 copy.122
  87.0 0.2 copy.128
  87.2 6.9 %convolution_bitcast_fusion.3 = f32[32,1,128,128]{2,0,3,1:T(8,128)S(1)} fusion(bf16[4,32,256]{1,0,2:T(4,128)(2,1)} %copy.121, bf16[1,4,128,384]{2,1,3,0:T(4,128)(2,1)S(1)} %copy.118), kind=kOutput, calls=%fused_computation.14 | convolution fusion | flops 1073741824 | bytes 2555904 | tf_op jit(solution)/shard_map/conv_general_dilated | solution.py:38
  94.1 5.9 %convolution_bitcast_fusion.1 = f32[32,1,128,128]{2,0,3,1:T(8,128)S(1)} fusion(bf16[4,32,256]{1,0,2:T(4,128)(2,1)S(1)} %copy.127, bf16[1,4,128,384]{2,1,3,0:T(4,128)(2,1)S(1)} %copy.125), kind=kOutput, calls=%fused_computation.12 | convolution fusion | flops 1073741824 | bytes 2555904 | tf_op jit(solution)/shard_map/conv_general_dilated | solution.py:38
  99.9 6.1 %convolution_bitcast_fusion.2 = f32[32,1,128,128]{2,0,3,1:T(8,128)S(1)} fusion(bf16[4,32,256]{1,0,2:T(4,128)(2,1)S(1)} %copy.124, bf16[1,4,128,384]{2,1,3,0:T(4,128)(2,1)S(1)} %copy.122), kind=kOutput, calls=%fused_computation.13 | convolution fusion | flops 1073741824 | bytes 2555904 | tf_op jit(solution)/shard_map/conv_general_dilated | solution.py:38
  106.0 5.9 %convolution_bitcast_fusion = f32[32,1,128,128]{2,0,3,1:T(8,128)S(1)} fusion(bf16[4,32,256]{1,0,2:T(4,128)(2,1)S(1)} %copy.130, bf16[1,4,128,384]{2,1,3,0:T(4,128)(2,1)S(1)} %copy.128), kind=kOutput, calls=%fused_computation.11 | convolution fusion | flops 1073741824 | bytes 2555904 | tf_op jit(solution)/shard_map/conv_general_dilated | solution.py:38
  111.9 4.1 %maximum_multiply_fusion = f32[32,4,128,128]{2,0,3,1:T(8,128)} fusion(f32[32,1,128,128]{2,0,3,1:T(8,128)S(1)} %convolution_bitcast_fusion, f32[32,1,128,128]{2,0,3,1:T(8,128)S(1)} %convolution_bitcast_fusion.1, f32[32,1,128,128]{2,0,3,1:T(8,128)S(1)} %convolution_bitcast_fusion.2, f32[32,1,128,128]{2,0,3,1:T(8,128)S(1)} %convolution_bitcast_fusion.3, ...), kind=kLoop, calls=%fused_computation.2 | loop fusion | flops 8388608 | bytes 16777232 | tf_op jit(solution)/shard_map/mul | solution.py:78
  116.0 9.9 %copy.112 = f32[32,4,128,128]{3,2,1,0:T(8,128)} copy(f32[32,4,128,128]{2,0,3,1:T(8,128)} %maximum_multiply_fusion) | data formatting | bytes 16777216 | tf_op jit(solution)/shard_map/mul | solution.py:78
  (11 shorter events, 0.1 us)
Async XLA Ops:
  6.5 5.4 %copy-start = (bf16[1,320,2,512]{3,2,1,0:T(2,128)(2,1)S(1)}, bf16[1,320,2,512]{3,2,1,0:T(2,128)(2,1)}, u32[]{:S(2)}) copy-start(bf16[1,320,2,512]{3,2,1,0:T(2,128)(2,1)} %param.4) | copy-start | bytes 1966084
  6.5 1.7 %copy-start.1 = (s32[320]{0:T(512)S(1)}, s32[320]{0:T(512)}, u32[]{:S(2)}) copy-start(s32[320]{0:T(512)} %param.6) | copy-start | bytes 3844
  6.5 78.1 %all-gather.2.cloned.1.call-start = ((), (), s32[]{:S(2)}) async-start(), calls=%async_computation.2 | async-start | bytes 1966080 | tf_op jit(solution)/shard_map/all_gather | solution.py:73
  57.1 6.0 %copy-start.2 = (s32[64,4,2]{0,2,1:T(2,128)S(1)}, s32[64,4,2]{0,2,1:T(2,128)}, u32[]{:S(2)}) copy-start(s32[64,4,2]{0,2,1:T(2,128)} %param.5) | copy-start | bytes 6148
  58.9 10.7 %all-to-all-start.1 = ((bf16[4,1,128,384]{3,0,1,2:T(4,128)(2,1)}), bf16[4,1,128,384]{3,0,1,2:T(4,128)(2,1)S(1)}, u32[]{:S(2)}, u32[]{:S(2)}) async-start(bf16[4,1,128,384]{3,0,1,2:T(4,128)(2,1)} %copy.99), calls=%async_computation.1 | async-start | bytes 786432 | tf_op jit(solution)/shard_map/all_to_all | solution.py:71
Sparse Core Ops, SparseCore 0:
  58.0 26.5 all-gather.1
where the time goes:
time: 133 us
  blocking collectives  35.5 us (27%)
  local copies, waits for them, and re-layouts  27.8 us (21%)
  matrix products  26.5 us (20%)
  waiting for transfers between devices  19 us (14%)
  between operations  14.4 us (11%)
  other arithmetic  5.36 us (4%)
  starting transfers between devices  4.18 us (3%)
    all_to_all x1, blocking collectives, body(): lax.all_to_all(outgoing, 'pairs', split_axis=0, concat_axis=2, tiled=True)  35.5 us
    conv_general_dilated x4, matrix products, correlate(): lax.conv_general_dilated(source, kernel, (1,), 'VALID', dimension_numbers...  24.7 us
    all_gather x1, waiting for transfers between devices, body(): piece = lax.all_gather(seconds[:, None], 'win', axis=1, tiled=True)  12.6 us
    mul x1, local copies, waits for them, and re-layouts, body(): return summed * scale * tile_valid[None, :, None, None]  9.9 us
    all_to_all x1, waiting for transfers between devices, body(): lax.all_to_all(firsts[:, None], 'win', split_axis=2, concat_axis=1, tiled...  6.37 us
    all_to_all x1, starting transfers between devices, body(): lax.all_to_all(firsts[:, None], 'win', split_axis=2, concat_axis=1, tiled...  4.18 us
    mul x2, other arithmetic, body(): return summed * scale * tile_valid[None, :, None, None]  4.14 us
    gather x2, local copies, waits for them, and re-layouts, body(): slot_index = block_slot[jnp.maximum(wanted, 0)]  3.57 us
  transfers between devices with their start and end apart: 2, of which 2 were waited for; matrix products, arithmetic and copies ran while one was open for 3% of the time, Pallas kernels for 0%

commit v1 on v0

--- a/solution.py
+++ b/solution.py
@@ -70,7 +70,9 @@
     row_share = channels // win_count
     spread_rows = lax.all_to_all(firsts[:, None], "win", split_axis=2, concat_axis=1, tiled=True)
     initial = jnp.zeros((row_share, tile_count, channels, LAGS), jnp.float32)
-    piece = lax.all_gather(seconds[:, None], "win", axis=1, tiled=True)
+    piece = jnp.concatenate(
+        lax.all_to_all(jnp.stack([seconds[:, None]] * lax.axis_size("win")), "win", 0, 0), axis=1
+    )
     summed = initial + jnp.stack(
         [correlate(spread_rows[tile], piece[tile]) for tile in range(tile_count)], 1
     )

time: 133 us -> 128 us (0.962)
  the two profiles are of different devices: /device:TPU:1 before, /device:TPU:32 now
where the time goes in v1:
time: 128 us; the launch traced here: 127 us
  blocking collectives  33.7 us (26%)
  local copies, waits for them, and re-layouts  27.5 us (21%)
  matrix products  25.8 us (20%)
  waiting for transfers between devices  25.6 us (20%)
  starting transfers between devices  8.21 us (6%)
  other arithmetic  5.36 us (4%)
    all_to_all x1, blocking collectives, body(): lax.all_to_all(outgoing, 'pairs', split_axis=0, concat_axis=2, tiled=True)  33.7 us
    conv_general_dilated x4, matrix products, correlate(): lax.conv_general_dilated(source, kernel, (1,), 'VALID', dimension_numbers...  23.9 us
    all_to_all x1, waiting for transfers between devices, body(): lax.all_to_all(jnp.stack([seconds[:, None]] * lax.axis_size('win')), 'win...  18.1 us
    mul x1, local copies, waits for them, and re-layouts, body(): return summed * scale * tile_valid[None, :, None, None]  9.9 us
    all_to_all x1, waiting for transfers between devices, body(): lax.all_to_all(firsts[:, None], 'win', split_axis=2, concat_axis=1, tiled...  7.5 us
    all_to_all x1, starting transfers between devices, body(): lax.all_to_all(firsts[:, None], 'win', split_axis=2, concat_axis=1, tiled...  4.46 us
    mul x2, other arithmetic, body(): return summed * scale * tile_valid[None, :, None, None]  4.13 us
    all_to_all x1, starting transfers between devices, body(): lax.all_to_all(jnp.stack([seconds[:, None]] * lax.axis_size('win')), 'win...  3.74 us
  transfers between devices with their start and end apart: 2, of which 2 were waited for; matrix products, arithmetic and copies ran while one was open for 2% of the time, Pallas kernels for 0%

profile of v1, /device:TPU:32, one launch (start us, length us, event | category | flops | bytes accessed | tf_op | source)
XLA Modules:
  0.0 127.2 jit_solution(10189922814773484724)
XLA Ops:
  0.0 0.0 copy-start
  0.0 0.0 copy-start.1
  0.7 0.7 broadcast_maximum_fusion
  1.4 0.1 copy.81
  1.6 0.2 reshape.124
  1.7 0.0 copy-done.1
  1.8 3.5 %gather_fusion = s32[512]{0:T(512)S(1)} fusion(s32[320]{0:T(512)S(1)} %copy-done.1, s32[1024]{0:T(1024)S(1)} %pad_clamp_fusion.1), kind=kCustom, calls=%fused_computation | custom fusion | bytes 6144 | tf_op jit(solution)/shard_map/gather | solution.py:60
  5.3 0.1 reshape.123
  5.4 0.0 copy-done
  5.4 0.9 constant_dynamic-slice_fusion.1
  6.3 0.1 convert_abs_fusion
  6.4 0.4 copy.83
  6.8 0.4 copy.84
  7.1 0.1 pad_slice_fusion.1
  7.3 1.8 %fusion = f32[320,2,3,128]{0,3,2,1:T(8,128)S(1)} fusion(f32[320,2,3,128]{3,0,2,1:T(8,128)S(1)} %get-tuple-element.6, f32[320,2,3,128]{3,0,2,1:T(8,128)S(1)} %copy.84, f32[320,2,3,128]{3,0,2,1:T(8,128)S(1)} %get-tuple-element.5, s32[384]{0:T(512)S(1)} %iota_add_fusion), kind=kOutput, calls=%fused_computation.3 | convolution fusion | flops 1134084096 | bytes 3933696 | tf_op jit(solution)/shard_map/...ni,ij->...nj/dot_general | solution.py:22
  9.1 0.3 copy.87
  9.5 0.2 fusion.7
  9.7 0.5 copy.88
  10.2 3.1 %gather_fusion.1 = bf16[512,2,384]{2,1,0:T(2,128)(2,1)S(1)} fusion(bf16[320,2,384]{2,1,0:T(2,128)(2,1)S(1)} %copy.88, s32[1024]{0:T(1024)S(1)} %pad_clamp_fusion), kind=kCustom, calls=%fused_computation.1 | custom fusion | bytes 1574912 | tf_op jit(solution)/shard_map/jit(_take)/gather | solution.py:61
  13.3 0.2 bitcast_select_fusion
  13.5 0.1 copy.90
  13.6 33.7 %all_to_all.29 = bf16[64,8,2,384]{3,1,2,0:T(8,128)(2,1)S(1)} all-to-all(bf16[64,8,2,384]{3,1,2,0:T(8,128)(2,1)S(1)} %copy.90), channel_id=1, replica_groups=mesh['pairs'=64,'win'=4] {'pairs'}, dimensions={0} | all-to-all | bytes 1572864 | tf_op jit(solution)/shard_map/all_to_all | solution.py:64
  47.3 0.3 reshape.142
  47.6 1.1 fusion.19
  48.7 0.9 copy.94
  49.6 4.5 %all-to-all-start.2 = ((bf16[4,1,128,384]{3,0,1,2:T(4,128)(2,1)}), bf16[4,1,128,384]{3,0,1,2:T(4,128)(2,1)S(1)}, u32[]{:S(2)}, u32[]{:S(2)}) async-start(bf16[4,1,128,384]{3,0,1,2:T(4,128)(2,1)} %copy.94), calls=%async_computation.2 | async-start | bytes 786432 | tf_op jit(solution)/shard_map/all_to_all | solution.py:71
  54.1 1.0 copy.120
  55.2 7.5 %all-to-all-done.2 = bf16[4,1,128,384]{3,0,1,2:T(4,128)(2,1)S(1)} async-done(((bf16[4,1,128,384]{3,0,1,2:T(4,128)(2,1)}), bf16[4,1,128,384]{3,0,1,2:T(4,128)(2,1)S(1)}, u32[]{:S(2)}, u32[]{:S(2)}) %all-to-all-start.2) | async-done | bytes 393248 | tf_op jit(solution)/shard_map/all_to_all | solution.py:71
  62.7 0.0 copy-start.2
  62.7 1.4 %stack.18 = bf16[4,4,1,128,384]{3,4,2,1,0:T(8,128)(2,1)} broadcast(bf16[4,128,384]{1,2,0:T(8,128)(2,1)S(1)} %bitcast.70), dimensions={1,3,4} | broadcast | bytes 1966080 | tf_op jit(solution)/shard_map/stack | solution.py:74
  64.1 3.7 %all-to-all-start.1 = ((bf16[4,4,1,128,384]{3,4,2,1,0:T(8,128)(2,1)}), bf16[4,4,1,128,384]{3,4,2,1,0:T(8,128)(2,1)S(1)}, u32[]{:S(2)}, u32[]{:S(2)}) async-start(bf16[4,4,1,128,384]{3,4,2,1,0:T(8,128)(2,1)} %stack.18), calls=%async_computation.1 | async-start | bytes 3145728 | tf_op jit(solution)/shard_map/all_to_all | solution.py:74
  67.9 0.0 copy-done.2
  67.9 0.1 constant_dynamic-slice_fusion
  68.0 0.1 copy.103
  68.1 0.6 fusion.20
  68.7 0.1 slice.93
  68.8 0.1 slice.99
  68.9 0.1 slice.96
  69.0 0.1 slice.102
  69.1 0.2 copy.118
  69.3 0.2 copy.114
  69.5 0.2 copy.116
  69.7 0.2 copy.112
  69.9 18.1 %all-to-all-done.1 = bf16[4,4,1,128,384]{3,4,2,1,0:T(8,128)(2,1)S(1)} async-done(((bf16[4,4,1,128,384]{3,4,2,1,0:T(8,128)(2,1)}), bf16[4,4,1,128,384]{3,4,2,1,0:T(8,128)(2,1)S(1)}, u32[]{:S(2)}, u32[]{:S(2)}) %all-to-all-start.1) | async-done | bytes 1572896 | tf_op jit(solution)/shard_map/all_to_all | solution.py:74
  88.0 1.2 copy.125
  89.2 5.9 %convolution_bitcast_fusion = f32[32,1,128,128]{2,0,3,1:T(8,128)S(1)} fusion(bf16[4,32,256]{1,0,2:T(4,128)(2,1)S(1)} %copy.118, bf16[4,4,1,128,384]{3,1,4,2,0:T(4,128)(2,1)S(1)} %bitcast.66), kind=kOutput, calls=%fused_computation.11 | convolution fusion | flops 1073741824 | bytes 2752512 | tf_op jit(solution)/shard_map/conv_general_dilated | solution.py:38
  95.2 5.9 %convolution_bitcast_fusion.1 = f32[32,1,128,128]{2,0,3,1:T(8,128)S(1)} fusion(bf16[4,32,256]{1,0,2:T(4,128)(2,1)S(1)} %copy.116, bf16[4,4,1,128,384]{3,1,4,2,0:T(4,128)(2,1)S(1)} %bitcast.67), kind=kOutput, calls=%fused_computation.12 | convolution fusion | flops 1073741824 | bytes 2752512 | tf_op jit(solution)/shard_map/conv_general_dilated | solution.py:38
  101.1 6.1 %convolution_bitcast_fusion.2 = f32[32,1,128,128]{2,0,3,1:T(8,128)S(1)} fusion(bf16[4,32,256]{1,0,2:T(4,128)(2,1)S(1)} %copy.114, bf16[4,4,1,128,384]{3,1,4,2,0:T(4,128)(2,1)S(1)} %bitcast.68), kind=kOutput, calls=%fused_computation.13 | convolution fusion | flops 1073741824 | bytes 2752512 | tf_op jit(solution)/shard_map/conv_general_dilated | solution.py:38
  107.2 5.9 %convolution_bitcast_fusion.3 = f32[32,1,128,128]{2,0,3,1:T(8,128)S(1)} fusion(bf16[4,32,256]{1,0,2:T(4,128)(2,1)S(1)} %copy.112, bf16[4,4,1,128,384]{3,1,4,2,0:T(4,128)(2,1)S(1)} %bitcast.69), kind=kOutput, calls=%fused_computation.14 | convolution fusion | flops 1073741824 | bytes 2752512 | tf_op jit(solution)/shard_map/conv_general_dilated | solution.py:38
  113.1 4.1 %maximum_multiply_fusion = f32[32,4,128,128]{2,0,3,1:T(8,128)} fusion(f32[32,1,128,128]{2,0,3,1:T(8,128)S(1)} %convolution_bitcast_fusion, f32[32,1,128,128]{2,0,3,1:T(8,128)S(1)} %convolution_bitcast_fusion.1, f32[32,1,128,128]{2,0,3,1:T(8,128)S(1)} %convolution_bitcast_fusion.2, f32[32,1,128,128]{2,0,3,1:T(8,128)S(1)} %convolution_bitcast_fusion.3, ...), kind=kLoop, calls=%fused_computation.2 | loop fusion | flops 8388608 | bytes 16777232 | tf_op jit(solution)/shard_map/mul | solution.py:80
  117.3 9.9 %copy.104 = f32[32,4,128,128]{3,2,1,0:T(8,128)} copy(f32[32,4,128,128]{2,0,3,1:T(8,128)} %maximum_multiply_fusion) | data formatting | bytes 16777216 | tf_op jit(solution)/shard_map/mul | solution.py:80
  (11 shorter events, 0.1 us)
Async XLA Ops:
  0.0 5.4 %copy-start = (bf16[1,320,2,512]{3,2,1,0:T(2,128)(2,1)S(1)}, bf16[1,320,2,512]{3,2,1,0:T(2,128)(2,1)}, u32[]{:S(2)}) copy-start(bf16[1,320,2,512]{3,2,1,0:T(2,128)(2,1)} %param.4) | copy-start | bytes 1966084
  0.0 1.7 %copy-start.1 = (s32[320]{0:T(512)S(1)}, s32[320]{0:T(512)}, u32[]{:S(2)}) copy-start(s32[320]{0:T(512)} %param.6) | copy-start | bytes 3844
  49.6 13.0 %all-to-all-start.2 = ((bf16[4,1,128,384]{3,0,1,2:T(4,128)(2,1)}), bf16[4,1,128,384]{3,0,1,2:T(4,128)(2,1)S(1)}, u32[]{:S(2)}, u32[]{:S(2)}) async-start(bf16[4,1,128,384]{3,0,1,2:T(4,128)(2,1)} %copy.94), calls=%async_computation.2 | async-start | bytes 786432 | tf_op jit(solution)/shard_map/all_to_all | solution.py:71
  62.7 5.2 %copy-start.2 = (s32[64,4,2]{0,2,1:T(2,128)S(1)}, s32[64,4,2]{0,2,1:T(2,128)}, u32[]{:S(2)}) copy-start(s32[64,4,2]{0,2,1:T(2,128)} %param.5) | copy-start | bytes 6148
  64.1 23.9 %all-to-all-start.1 = ((bf16[4,4,1,128,384]{3,4,2,1,0:T(8,128)(2,1)}), bf16[4,4,1,128,384]{3,4,2,1,0:T(8,128)(2,1)S(1)}, u32[]{:S(2)}, u32[]{:S(2)}) async-start(bf16[4,4,1,128,384]{3,4,2,1,0:T(8,128)(2,1)} %stack.18), calls=%async_computation.1 | async-start | bytes 3145728 | tf_op jit(solution)/shard_map/all_to_all | solution.py:74
